TPU v7x, 512 devices: a whole 4x4x16 slice. The times are simulated.
512 devices in a mesh: dp: 32 (over z, x_hi), lon: 16 (over y, x_lo, core).
Axes of the slice: x: 4 (x_hi: 2, x_lo: 2; x = x_hi * 2 + x_lo), y: 4, z: 16, core: 2. Of those that a mesh axis runs over, the one named last changes fastest.
Arguments:
- fields: bfloat16 [32, 128, 48, 768], P('dp', 'lon'), may hold values from -6 to 6
- cotangent: bfloat16 [32, 128, 48, 768], P('dp', 'lon'), may hold values from -6 to 6
- first_weight: bfloat16 [2, 8, 96, 96], replicated, may hold values from -0.4375 to 0.4375
- second_weight: bfloat16 [2, 8, 96, 96], replicated, may hold values from -0.4375 to 0.4375
Outputs:
- layer_out: bfloat16 [32, 128, 48, 768], P('dp', 'lon')
- field_grad: bfloat16 [32, 128, 48, 768], P('dp', 'lon')
- first_grad: float32 [2, 8, 96, 96], replicated
- second_grad: float32 [2, 8, 96, 96], replicated
All inputs are finite; a program needn't handle non-finite values.
Results may differ from a plain program's by a relative error of at most 0.015.
Values may be sent and summed in bfloat16 or wider, within the bound.
A program may use at most 64 MiB of HBM per device.

v0:
```python
import math
import jax
import jax.numpy as jnp
from jax import lax
from jax.sharding import PartitionSpec as P

COEF = 0.7978845608028654
CUBIC = 0.044715


def gelu_value(inner):
    hyper = jnp.tanh(COEF * (inner + CUBIC * inner * inner * inner))
    return 0.5 * inner * (1.0 + hyper)


def gelu_slope(inner):
    hyper = jnp.tanh(COEF * (inner + CUBIC * inner * inner * inner))
    return 0.5 * (1.0 + hyper) + 0.5 * inner * (1.0 - hyper * hyper) * COEF * (
        1.0 + 3.0 * CUBIC * inner * inner
    )


def make_basis(length, count):
    cell_idx = jnp.arange(length, dtype=jnp.int32)
    mode_idx = jnp.arange(count, dtype=jnp.int32)
    product = cell_idx[:, None] * mode_idx[None, :] % length
    angle = product.astype(jnp.float32) * jnp.float32(2.0 * math.pi / length)
    return jnp.stack([jnp.cos(angle), -jnp.sin(angle)], axis=-1).astype(jnp.bfloat16)


def lat_apply(spec, table, lat_scale):
    return (
        jnp.einsum("kphc,phqj->kqjc", spec, table, preferred_element_type=jnp.float32) * lat_scale
    ).astype(jnp.bfloat16)


def forward_weight(weight):
    return jnp.stack([jnp.stack([weight[0], weight[1]]), jnp.stack([-weight[1], weight[0]])])


def adjoint_weight(weight):
    return jnp.stack([jnp.stack([weight[0], -weight[1]]), jnp.stack([weight[1], weight[0]])])


def block_product(spec, stacked):
    return jnp.einsum("kphbi,pqbij->kqhbj", spec, stacked, preferred_element_type=jnp.float32)


def block_adjoint(spec, stacked):
    return jnp.einsum("kphbj,pqbij->kqhbi", spec, stacked, preferred_element_type=jnp.float32)


def block_outer(left, right):
    pairs = jnp.einsum("kphbi,kqhbj->pqbij", left, right, preferred_element_type=jnp.float32)
    return jnp.stack([pairs[0, 0] + pairs[1, 1], pairs[0, 1] - pairs[1, 0]])


def on_device(fields, cotangent, first_weight, second_weight):
    cell_rows = fields[0]
    cot_rows = cotangent[0]
    lat_rows = cell_rows.shape[1]
    channels = cell_rows.shape[2]
    groups = first_weight.shape[1]
    group_width = first_weight.shape[2]
    lon_count = lax.axis_size("lon")
    total_cells = cell_rows.shape[0] * lon_count
    dft_basis = make_basis(total_cells, total_cells // 2)
    lat_basis = make_basis(lat_rows, lat_rows)
    cos_tab = lat_basis[:, :, 0]
    sin_tab = lat_basis[:, :, 1]
    lat_fwd_table = jnp.stack(
        [jnp.stack([cos_tab, sin_tab], axis=1), jnp.stack([-sin_tab, cos_tab], axis=1)], axis=0
    )
    lat_inv_table = jnp.stack(
        [jnp.stack([cos_tab.T, -sin_tab.T], axis=1), jnp.stack([sin_tab.T, cos_tab.T], axis=1)],
        axis=0,
    )
    norm_scale = 1.0 / math.sqrt(total_cells)
    lat_scale = 1.0 / math.sqrt(lat_rows)
    local_modes = cell_rows.shape[0] // 2
    mode_idx = lax.axis_index("lon") * local_modes + jnp.arange(local_modes, dtype=jnp.int32)
    mode_weight = jnp.where(mode_idx == 0, 1.0, 2.0).astype(jnp.bfloat16)[:, None, None, None]
    first_fwd = forward_weight(first_weight)
    second_fwd = forward_weight(second_weight)
    first_adj = adjoint_weight(first_weight)
    second_adj = adjoint_weight(second_weight)

    def local_dft(all_lines):
        return (
            jnp.einsum("whc,wkp->kphc", all_lines, dft_basis, preferred_element_type=jnp.float32)
            * norm_scale
        ).astype(jnp.bfloat16)

    def local_idft(all_modes):
        return (
            jnp.einsum("kphc,wkp->whc", all_modes, dft_basis, preferred_element_type=jnp.float32)
            * norm_scale
        ).astype(jnp.bfloat16)

    def lines_to_modes(all_lines):
        return lax.all_to_all(local_dft(all_lines), "lon", split_axis=0, concat_axis=3, tiled=True)

    def modes_to_lines(all_modes):
        return lax.all_to_all(local_idft(all_modes), "lon", split_axis=0, concat_axis=2, tiled=True)

    def to_spectrum(grid_rows):
        return lines_to_modes(
            lax.all_to_all(grid_rows, "lon", split_axis=2, concat_axis=0, tiled=True)
        )

    def to_cells(spec_rows):
        return modes_to_lines(
            lax.all_to_all(spec_rows, "lon", split_axis=3, concat_axis=0, tiled=True)
        )

    def split_groups(spec_rows):
        return spec_rows.reshape(local_modes, 2, lat_rows, groups, group_width)

    def join_groups(spec_rows):
        return spec_rows.astype(jnp.bfloat16).reshape(local_modes, 2, lat_rows, channels)

    lon_spec = to_spectrum(cell_rows)
    spectrum = split_groups(lat_apply(lon_spec, lat_fwd_table, lat_scale))
    inner = block_product(spectrum, first_fwd)
    act = gelu_value(inner).astype(jnp.bfloat16)
    mixed = join_groups(block_product(act, second_fwd)) * mode_weight
    mixed_lon = lat_apply(mixed, lat_inv_table, lat_scale)
    wave = to_cells(mixed_lon)
    dual_lon = to_spectrum(cot_rows)
    dual = split_groups(lat_apply(dual_lon, lat_fwd_table, lat_scale) * mode_weight)
    back = block_adjoint(dual, second_adj)
    pre = (back * gelu_slope(inner)).astype(jnp.bfloat16)
    back_spec = join_groups(block_adjoint(pre, first_adj))
    back_lon = lat_apply(back_spec, lat_inv_table, lat_scale)
    pull = to_cells(back_lon)
    layer_out = (cell_rows.astype(jnp.float32) + wave.astype(jnp.float32)).astype(jnp.bfloat16)
    field_grad = (cot_rows.astype(jnp.float32) + pull.astype(jnp.float32)).astype(jnp.bfloat16)
    sample_count = lax.axis_size("dp")
    second_term = block_outer(act, dual) / sample_count
    first_term = block_outer(spectrum, pre) / sample_count
    first_grad, second_grad = lax.psum((first_term, second_term), ("dp", "lon"))
    return (layer_out[None], field_grad[None], first_grad, second_grad)


def solution(mesh):
    placed = (P("dp", "lon", None, None), P("dp", "lon", None, None), P(), P())
    return jax.shard_map(
        on_device,
        mesh=mesh,
        in_specs=placed,
        out_specs=(P("dp", "lon", None, None), P("dp", "lon", None, None), P(), P()),
        check_vma=False,
    )
```

profile of v0, /device:TPU:1, one launch (start us, length us, event | category | flops | bytes accessed | tf_op | source)
XLA Modules:
  0.0 643.6 jit_solution(1187848861176454927)
XLA Ops:
  7.2 2.0 copy.123
  9.3 3.1 reshape.309
  12.4 11.0 %all-to-all-start = ((bf16[16,2,9216]{2,1,0:T(2,128)(2,1)}), bf16[16,2,9216]{2,1,0:T(2,128)(2,1)}, u32[]{:S(2)}, u32[]{:S(2)}) async-start(bf16[16,2,9216]{2,1,0:T(2,128)(2,1)} %reshape.309), calls=%async_computation | async-start | bytes 1179648 | tf_op jit(solution)/shard_map/all_to_all | solution.py:108
  24.6 3.1 reshape.317
  30.0 4.0 all-to-all-done
  34.1 5.2 all-to-all-start.4
  40.8 2.4 reshape.310
  45.8 1.4 copy.126
  47.2 3.1 reshape.311
  50.3 6.4 %all-to-all-start.1 = ((bf16[16,2,9216]{2,1,0:T(2,128)(2,1)}), bf16[16,2,9216]{2,1,0:T(2,128)(2,1)}, u32[]{:S(2)}, u32[]{:S(2)}) async-start(bf16[16,2,9216]{2,1,0:T(2,128)(2,1)} %reshape.311), calls=%async_computation.1 | async-start | bytes 1179648 | tf_op jit(solution)/shard_map/all_to_all | solution.py:101
  59.0 2.4 reshape.318
  64.0 1.4 copy.140
  65.4 3.1 reshape.319
  68.5 5.9 all-to-all-start.5
  77.1 2.4 reshape.312
  80.6 1.6 reshape.275
  83.4 1.6 all-to-all-done.5
  85.0 2.4 reshape.320
  87.5 2.2 copy.141
  89.7 2.9 reshape.288
  94.9 1.6 convolution_bitcast_fusion
  101.3 3.1 reshape.321
  104.4 4.5 all-to-all-start.6
  108.9 1.7 fusion.37
  113.5 2.2 copy.132
  115.7 4.1 reshape.313
  119.9 1.4 fusion.69
  121.4 5.8 all-to-all-start.2
  129.2 1.8 reshape.322
  132.3 1.5 fusion.30
  133.8 1.8 copy.151
  135.6 3.1 reshape.323
  138.7 5.7 all-to-all-start.7
  144.4 2.4 reshape.314
  148.1 1.5 fusion.27
  149.6 1.8 copy.135
  151.4 3.1 reshape.315
  154.5 451.1 %all-reduce.3.cloned.1.call-done = (f32[2,8,96,96]{2,3,1,0:T(8,128)}, f32[2,8,96,96]{2,3,1,0:T(8,128)}) async-done(((f32[2,8,96,96]{2,3,1,0:T(8,128)}, f32[2,8,96,96]{2,3,1,0:T(8,128)}), (f32[2,8,96,96]{2,3,1,0:T(8,128)}, f32[2,8,96,96]{2,3,1,0:T(8,128)})) %all-reduce.3.cloned.1.call-update) | async-done | bytes 1179664 | tf_op jit(solution)/shard_map/psum | solution.py:141
  605.7 2.4 copy.158
  609.2 7.4 %all-to-all-start.3 = ((bf16[16,2,9216]{2,1,0:T(2,128)(2,1)}), bf16[16,2,9216]{2,1,0:T(2,128)(2,1)}, u32[]{:S(2)}, u32[]{:S(2)}) async-start(bf16[16,2,9216]{2,1,0:T(2,128)(2,1)} %reshape.315), calls=%async_computation.3 | async-start | bytes 1179648 | tf_op jit(solution)/shard_map/all_to_all | solution.py:104
  616.6 2.4 reshape.324
  619.4 1.8 copy.152
  621.2 2.2 reshape.269
  623.5 2.3 add_convert_fusion
  627.1 2.4 reshape.316
  629.9 1.8 copy.136
  631.7 2.2 reshape.268
  634.0 2.3 add_convert_fusion.1
  (123 shorter events, 34.8 us)
Async XLA Ops:
  12.3 11.0 %copy-start = (bf16[1,8,48,768]{3,2,1,0:T(8,128)(2,1)S(1)}, bf16[1,8,48,768]{3,2,1,0:T(8,128)(2,1)}, u32[]{:S(2)}) copy-start(bf16[1,8,48,768]{3,2,1,0:T(8,128)(2,1)} %param.5) | copy-start | bytes 1769476
  12.4 21.7 %all-to-all-start = ((bf16[16,2,9216]{2,1,0:T(2,128)(2,1)}), bf16[16,2,9216]{2,1,0:T(2,128)(2,1)}, u32[]{:S(2)}, u32[]{:S(2)}) async-start(bf16[16,2,9216]{2,1,0:T(2,128)(2,1)} %reshape.309), calls=%async_computation | async-start | bytes 1179648 | tf_op jit(solution)/shard_map/all_to_all | solution.py:108
  24.6 15.4 %copy-start.21 = (bf16[2,8,96,96]{3,2,1,0:T(8,128)(2,1)S(1)}, bf16[2,8,96,96]{3,2,1,0:T(8,128)(2,1)}, u32[]{:S(2)}) copy-start(bf16[2,8,96,96]{3,2,1,0:T(8,128)(2,1)} %param.6) | copy-start | bytes 884740
  34.1 16.2 %all-to-all-start.4 = ((bf16[16,2,9216]{2,1,0:T(2,128)(2,1)}), bf16[16,2,9216]{2,1,0:T(2,128)(2,1)}, u32[]{:S(2)}, u32[]{:S(2)}) async-start(bf16[16,2,9216]{2,1,0:T(2,128)(2,1)} %reshape.317), calls=%async_computation.4 | async-start | bytes 1179648 | tf_op jit(solution)/shard_map/all_to_all | solution.py:108
  44.3 1.0 copy-start.14
  47.2 9.6 %copy-start.29 = (bf16[48,1,48]{2,0,1:T(8,128)(2,1)S(1)}, bf16[48,1,48]{2,0,1:T(8,128)(2,1)}, u32[]{:S(2)}) copy-start(bf16[48,1,48]{2,0,1:T(8,128)(2,1)} %get-tuple-element.48) | copy-start | bytes 13828
  47.2 9.6 %copy-start.30 = (bf16[48,1,48]{2,0,1:T(8,128)(2,1)S(1)}, bf16[48,1,48]{2,0,1:T(8,128)(2,1)}, u32[]{:S(2)}) copy-start(bf16[48,1,48]{2,0,1:T(8,128)(2,1)} %get-tuple-element.49) | copy-start | bytes 13828
  47.2 9.6 %copy-start.31 = (bf16[48,1,48]{2,0,1:T(8,128)(2,1)S(1)}, bf16[48,1,48]{2,0,1:T(8,128)(2,1)}, u32[]{:S(2)}) copy-start(bf16[48,1,48]{2,0,1:T(8,128)(2,1)} %fusion.91) | copy-start | bytes 13828
  47.2 10.2 %copy-start.22 = (bf16[2,8,96,96]{3,2,1,0:T(8,128)(2,1)S(1)}, bf16[2,8,96,96]{3,2,1,0:T(8,128)(2,1)}, u32[]{:S(2)}) copy-start(bf16[2,8,96,96]{3,2,1,0:T(8,128)(2,1)} %param.7) | copy-start | bytes 884740
  50.3 18.2 %all-to-all-start.1 = ((bf16[16,2,9216]{2,1,0:T(2,128)(2,1)}), bf16[16,2,9216]{2,1,0:T(2,128)(2,1)}, u32[]{:S(2)}, u32[]{:S(2)}) async-start(bf16[16,2,9216]{2,1,0:T(2,128)(2,1)} %reshape.311), calls=%async_computation.1 | async-start | bytes 1179648 | tf_op jit(solution)/shard_map/all_to_all | solution.py:101
  57.5 0.7 copy-start.2
  62.5 1.0 copy-start.15
  65.4 9.5 %copy-start.8 = (bf16[1,8,96,96]{3,2,0,1:T(8,128)(2,1)S(1)}, bf16[1,8,96,96]{3,2,0,1:T(8,128)(2,1)}, u32[]{:S(2)}) copy-start(bf16[1,8,96,96]{3,2,0,1:T(8,128)(2,1)} %get-tuple-element.26) | copy-start | bytes 442372
  65.4 9.5 %copy-start.9 = (bf16[1,8,96,96]{3,2,0,1:T(8,128)(2,1)S(1)}, bf16[1,8,96,96]{3,2,0,1:T(8,128)(2,1)}, u32[]{:S(2)}) copy-start(bf16[1,8,96,96]{3,2,0,1:T(8,128)(2,1)} %get-tuple-element.27) | copy-start | bytes 442372
  65.4 9.5 %copy-start.10 = (bf16[1,8,96,96]{3,2,0,1:T(8,128)(2,1)S(1)}, bf16[1,8,96,96]{3,2,0,1:T(8,128)(2,1)}, u32[]{:S(2)}) copy-start(bf16[1,8,96,96]{3,2,0,1:T(8,128)(2,1)} %get-tuple-element.28) | copy-start | bytes 442372
  68.5 7.5 %copy-start.11 = (bf16[1,8,96,96]{3,2,0,1:T(8,128)(2,1)S(1)}, bf16[1,8,96,96]{3,2,0,1:T(8,128)(2,1)}, u32[]{:S(2)}) copy-start(bf16[1,8,96,96]{3,2,0,1:T(8,128)(2,1)} %get-tuple-element.31) | copy-start | bytes 442372
  68.5 7.5 %copy-start.12 = (bf16[1,8,96,96]{3,2,0,1:T(8,128)(2,1)S(1)}, bf16[1,8,96,96]{3,2,0,1:T(8,128)(2,1)}, u32[]{:S(2)}) copy-start(bf16[1,8,96,96]{3,2,0,1:T(8,128)(2,1)} %get-tuple-element.32) | copy-start | bytes 442372
  68.5 7.5 %copy-start.13 = (bf16[1,8,96,96]{3,2,0,1:T(8,128)(2,1)S(1)}, bf16[1,8,96,96]{3,2,0,1:T(8,128)(2,1)}, u32[]{:S(2)}) copy-start(bf16[1,8,96,96]{3,2,0,1:T(8,128)(2,1)} %get-tuple-element.33) | copy-start | bytes 442372
  68.5 16.5 %all-to-all-start.5 = ((bf16[16,2,9216]{2,1,0:T(2,128)(2,1)}), bf16[16,2,9216]{2,1,0:T(2,128)(2,1)}, u32[]{:S(2)}, u32[]{:S(2)}) async-start(bf16[16,2,9216]{2,1,0:T(2,128)(2,1)} %reshape.319), calls=%async_computation.5 | async-start | bytes 1179648 | tf_op jit(solution)/shard_map/all_to_all | solution.py:101
  80.6 1.6 copy-start.25
  80.6 1.6 copy-start.27
  89.7 2.9 copy-start.26
  89.7 2.9 copy-start.28
  89.7 2.9 copy-start.32
  92.6 1.2 copy-start.1
  94.8 1.7 copy-start.7
  94.8 1.7 copy-start.19
  94.8 1.6 copy-start.20
  96.5 1.3 copy-start.17
  96.5 1.3 copy-start.18
  97.8 0.9 copy-start.5
  98.7 1.2 copy-start.23
  98.7 1.2 copy-start.24
  101.3 7.6 %copy-start.3 = (bf16[2,8,96,96]{3,2,0,1:T(8,128)(2,1)S(1)}, bf16[2,8,96,96]{3,2,0,1:T(8,128)(2,1)}, u32[]{:S(2)}) copy-start(bf16[2,8,96,96]{3,2,0,1:T(8,128)(2,1)} %copy-done.2) | copy-start | bytes 884740
  104.4 17.0 %all-to-all-start.6 = ((bf16[16,2,9216]{2,1,0:T(2,128)(2,1)}), bf16[16,2,9216]{2,1,0:T(2,128)(2,1)S(1)}, u32[]{:S(2)}, u32[]{:S(2)}) async-start(bf16[16,2,9216]{2,1,0:T(2,128)(2,1)} %reshape.321), calls=%async_computation.6 | async-start | bytes 1179648 | tf_op jit(solution)/shard_map/all_to_all | solution.py:113
  111.8 1.2 copy-start.6
  121.4 17.3 %all-to-all-start.2 = ((bf16[16,2,9216]{2,1,0:T(2,128)(2,1)}), bf16[16,2,9216]{2,1,0:T(2,128)(2,1)}, u32[]{:S(2)}, u32[]{:S(2)}) async-start(bf16[16,2,9216]{2,1,0:T(2,128)(2,1)} %reshape.313), calls=%async_computation.2 | async-start | bytes 1179648 | tf_op jit(solution)/shard_map/all_to_all | solution.py:113
  127.2 478.5 %all-reduce.3.cloned.1.call-start = ((), (), s32[]{:S(2)}) async-start(), calls=%async_computation.8 | async-start | bytes 3145728 | tf_op jit(solution)/shard_map/psum | solution.py:141
  131.0 1.2 copy-start.16
  138.7 470.5 %all-to-all-start.7 = ((bf16[16,2,9216]{2,1,0:T(2,128)(2,1)}), bf16[16,2,9216]{2,1,0:T(2,128)(2,1)}, u32[]{:S(2)}, u32[]{:S(2)}) async-start(bf16[16,2,9216]{2,1,0:T(2,128)(2,1)} %reshape.323), calls=%async_computation.7 | async-start | bytes 1179648 | tf_op jit(solution)/shard_map/all_to_all | solution.py:104
  605.7 2.4 copy-start.4
  609.2 17.9 %all-to-all-start.3 = ((bf16[16,2,9216]{2,1,0:T(2,128)(2,1)}), bf16[16,2,9216]{2,1,0:T(2,128)(2,1)}, u32[]{:S(2)}, u32[]{:S(2)}) async-start(bf16[16,2,9216]{2,1,0:T(2,128)(2,1)} %reshape.315), calls=%async_computation.3 | async-start | bytes 1179648 | tf_op jit(solution)/shard_map/all_to_all | solution.py:104
Sparse Core Ops, SparseCore 0:
  133.9 471.6 all-reduce.2
where the time goes:
time: 652 us; the launch traced here: 644 us
  waiting for transfers between devices  458 us (70%)
  local copies, waits for them, and re-layouts  88.6 us (14%)
  starting transfers between devices  52 us (8%)
  other arithmetic  17.4 us (3%)
  between operations  15.2 us (2%)
  matrix products  12.2 us (2%)
    psum x1, waiting for transfers between devices, on_device(): first_grad, second_grad = lax.psum((first_term, second_term), ('dp', 'lon'))  451 us
    unnamed x90, local copies, waits for them, and re-layouts  52.7 us
    all_to_all x2, starting transfers between devices, to_spectrum(): lax.all_to_all(grid_rows, 'lon', split_axis=2, concat_axis=0, tiled=True)  16.1 us
    all_to_all x2, starting transfers between devices, modes_to_lines(): lax.all_to_all(local_idft(all_modes), 'lon', split_axis=0, concat_axis=2,...  13.2 us
  transfers between devices with their start and end apart: 9, of which 4 were waited for; matrix products, arithmetic and copies ran while one was open for 13% of the time, Pallas kernels for 0%

commit v1 on v0

--- a/solution.py
+++ b/solution.py
@@ -138,7 +138,7 @@
     sample_count = lax.axis_size("dp")
     second_term = block_outer(act, dual) / sample_count
     first_term = block_outer(spectrum, pre) / sample_count
-    first_grad, second_grad = lax.psum((first_term, second_term), ("dp", "lon"))
+    first_grad, second_grad = lax.psum(lax.psum((first_term, second_term), "dp"), "lon")
     return (layer_out[None], field_grad[None], first_grad, second_grad)
 
 

time: 652 us -> 605 us (0.928)
  waiting for transfers between devices: 458 us -> 409 us
    psum x1 -> x2, waiting for transfers between devices: 451 us -> 401 us  [the longest x1 259 us: on_device(): lax.psum((first_term, second_term), 'dp')]
    unnamed x90 -> x98, local copies, waits for them, and re-layouts: 52.7 us -> 52 us
  transfers between devices with their start and end apart: 9 -> 10, of which waited for: 4 -> 5; matrix products, arithmetic and copies ran while one was open for 13% -> 15% of each run, Pallas kernels for 0% -> 0%
where the time goes in v1:
time: 605 us; the launch traced here: 597 us
  waiting for transfers between devices  409 us (68%)
  local copies, waits for them, and re-layouts  89.6 us (15%)
  starting transfers between devices  50.8 us (8%)
  other arithmetic  17.8 us (3%)
  between operations  15.3 us (3%)
  matrix products  14.4 us (2%)
    psum x1, waiting for transfers between devices, on_device(): lax.psum((first_term, second_term), 'dp')  259 us
    psum x1, waiting for transfers between devices, on_device(): lax.psum(lax.psum((first_term, second_term), 'dp'), 'lon')  142 us
    unnamed x98, local copies, waits for them, and re-layouts  52 us
    all_to_all x2, starting transfers between devices, to_spectrum(): lax.all_to_all(grid_rows, 'lon', split_axis=2, concat_axis=0, tiled=True)  16.1 us
    all_to_all x2, starting transfers between devices, lines_to_modes(): lax.all_to_all(local_dft(all_lines), 'lon', split_axis=0, concat_axis=3,...  12.3 us
  transfers between devices with their start and end apart: 10, of which 5 were waited for; matrix products, arithmetic and copies ran while one was open for 15% of the time, Pallas kernels for 0%

profile of v1, /device:TPU:1, one launch (start us, length us, event | category | flops | bytes accessed | tf_op | source)
XLA Modules:
  0.0 597.0 jit_solution(5755980012936249174)
XLA Ops:
  7.2 2.0 copy.123
  9.3 3.1 reshape.309
  12.4 11.0 %all-to-all-start = ((bf16[16,2,9216]{2,1,0:T(2,128)(2,1)}), bf16[16,2,9216]{2,1,0:T(2,128)(2,1)}, u32[]{:S(2)}, u32[]{:S(2)}) async-start(bf16[16,2,9216]{2,1,0:T(2,128)(2,1)} %reshape.309), calls=%async_computation | async-start | bytes 1179648 | tf_op jit(solution)/shard_map/all_to_all | solution.py:108
  24.6 3.1 reshape.317
  30.0 4.1 all-to-all-done
  34.1 5.2 all-to-all-start.4
  40.8 2.4 reshape.310
  47.2 3.1 reshape.311
  50.3 6.4 %all-to-all-start.1 = ((bf16[16,2,9216]{2,1,0:T(2,128)(2,1)}), bf16[16,2,9216]{2,1,0:T(2,128)(2,1)}, u32[]{:S(2)}, u32[]{:S(2)}) async-start(bf16[16,2,9216]{2,1,0:T(2,128)(2,1)} %reshape.311), calls=%async_computation.1 | async-start | bytes 1179648 | tf_op jit(solution)/shard_map/all_to_all | solution.py:101
  59.0 2.4 reshape.318
  65.4 3.1 reshape.319
  68.5 5.9 all-to-all-start.5
  77.1 2.4 reshape.312
  80.6 1.6 reshape.275
  83.4 1.6 all-to-all-done.5
  85.0 2.4 reshape.320
  87.5 2.2 copy.141
  89.7 2.9 reshape.288
  101.1 2.5 copy.148
  103.7 3.1 reshape.321
  106.7 5.1 all-to-all-start.6
  111.9 1.7 fusion.37
  116.1 3.0 convolution_bitcast_fusion
  119.1 2.5 copy.132
  121.6 3.1 reshape.313
  124.7 1.5 fusion.69
  126.2 5.8 all-to-all-start.2
  134.2 2.4 reshape.322
  137.9 1.5 fusion.30
  139.4 1.8 copy.151
  141.3 3.1 reshape.323
  144.4 5.7 all-to-all-start.7
  150.1 2.4 reshape.314
  153.8 1.5 fusion.27
  155.3 1.8 copy.135
  157.1 3.1 reshape.315
  160.2 2.0 all-to-all-done.7
  162.3 5.2 all-to-all-start.3
  167.7 2.5 reshape.324
  170.2 259.4 %all-reduce.5.cloned.1.call-done = (f32[2,8,96,96]{2,3,1,0:T(8,128)}, f32[2,8,96,96]{2,3,1,0:T(8,128)}) async-done(((f32[2,8,96,96]{2,3,1,0:T(8,128)}, f32[2,8,96,96]{2,3,1,0:T(8,128)}), (f32[2,8,96,96]{2,3,1,0:T(8,128)}, f32[2,8,96,96]{2,3,1,0:T(8,128)})) %all-reduce.5.cloned.1.call-update) | async-done | bytes 1179664 | tf_op jit(solution)/shard_map/psum | solution.py:141
  429.9 1.8 copy.152
  431.7 2.2 reshape.269
  434.0 2.4 reshape.316
  436.7 1.8 copy.136
  438.6 2.2 reshape.268
  440.8 2.5 add_convert_fusion
  444.2 142.0 %all-reduce.7.cloned.1.call-done = (f32[2,8,96,96]{2,3,1,0:T(8,128)}, f32[2,8,96,96]{2,3,1,0:T(8,128)}) async-done(((f32[2,8,96,96]{2,3,1,0:T(8,128)}, f32[2,8,96,96]{2,3,1,0:T(8,128)}), (f32[2,8,96,96]{2,3,1,0:T(8,128)}, f32[2,8,96,96]{2,3,1,0:T(8,128)})) %all-reduce.7.cloned.1.call-update) | async-done | bytes 1179664 | tf_op jit(solution)/shard_map/psum | solution.py:141
  586.2 2.4 copy.158
  (134 shorter events, 38.7 us)
Async XLA Ops:
  12.3 11.0 %copy-start.1 = (bf16[1,8,48,768]{3,2,1,0:T(8,128)(2,1)S(1)}, bf16[1,8,48,768]{3,2,1,0:T(8,128)(2,1)}, u32[]{:S(2)}) copy-start(bf16[1,8,48,768]{3,2,1,0:T(8,128)(2,1)} %param.5) | copy-start | bytes 1769476
  12.4 21.7 %all-to-all-start = ((bf16[16,2,9216]{2,1,0:T(2,128)(2,1)}), bf16[16,2,9216]{2,1,0:T(2,128)(2,1)}, u32[]{:S(2)}, u32[]{:S(2)}) async-start(bf16[16,2,9216]{2,1,0:T(2,128)(2,1)} %reshape.309), calls=%async_computation | async-start | bytes 1179648 | tf_op jit(solution)/shard_map/all_to_all | solution.py:108
  24.6 15.4 %copy-start.22 = (bf16[2,8,96,96]{3,2,1,0:T(8,128)(2,1)S(1)}, bf16[2,8,96,96]{3,2,1,0:T(8,128)(2,1)}, u32[]{:S(2)}) copy-start(bf16[2,8,96,96]{3,2,1,0:T(8,128)(2,1)} %param.6) | copy-start | bytes 884740
  34.1 16.2 %all-to-all-start.4 = ((bf16[16,2,9216]{2,1,0:T(2,128)(2,1)}), bf16[16,2,9216]{2,1,0:T(2,128)(2,1)}, u32[]{:S(2)}, u32[]{:S(2)}) async-start(bf16[16,2,9216]{2,1,0:T(2,128)(2,1)} %reshape.317), calls=%async_computation.4 | async-start | bytes 1179648 | tf_op jit(solution)/shard_map/all_to_all | solution.py:108
  44.3 1.0 copy-start.15
  47.2 9.6 %copy-start.32 = (bf16[48,1,48]{2,0,1:T(8,128)(2,1)S(1)}, bf16[48,1,48]{2,0,1:T(8,128)(2,1)}, u32[]{:S(2)}) copy-start(bf16[48,1,48]{2,0,1:T(8,128)(2,1)} %get-tuple-element.50) | copy-start | bytes 13828
  47.2 9.6 %copy-start.33 = (bf16[48,1,48]{2,0,1:T(8,128)(2,1)S(1)}, bf16[48,1,48]{2,0,1:T(8,128)(2,1)}, u32[]{:S(2)}) copy-start(bf16[48,1,48]{2,0,1:T(8,128)(2,1)} %get-tuple-element.51) | copy-start | bytes 13828
  47.2 9.6 %copy-start.34 = (bf16[48,1,48]{2,0,1:T(8,128)(2,1)S(1)}, bf16[48,1,48]{2,0,1:T(8,128)(2,1)}, u32[]{:S(2)}) copy-start(bf16[48,1,48]{2,0,1:T(8,128)(2,1)} %fusion.91) | copy-start | bytes 13828
  47.2 10.2 %copy-start.23 = (bf16[2,8,96,96]{3,2,1,0:T(8,128)(2,1)S(1)}, bf16[2,8,96,96]{3,2,1,0:T(8,128)(2,1)}, u32[]{:S(2)}) copy-start(bf16[2,8,96,96]{3,2,1,0:T(8,128)(2,1)} %param.7) | copy-start | bytes 884740
  50.3 18.2 %all-to-all-start.1 = ((bf16[16,2,9216]{2,1,0:T(2,128)(2,1)}), bf16[16,2,9216]{2,1,0:T(2,128)(2,1)}, u32[]{:S(2)}, u32[]{:S(2)}) async-start(bf16[16,2,9216]{2,1,0:T(2,128)(2,1)} %reshape.311), calls=%async_computation.1 | async-start | bytes 1179648 | tf_op jit(solution)/shard_map/all_to_all | solution.py:101
  57.4 0.8 copy-start.4
  62.5 1.0 copy-start.16
  65.4 9.5 %copy-start.9 = (bf16[1,8,96,96]{3,2,0,1:T(8,128)(2,1)S(1)}, bf16[1,8,96,96]{3,2,0,1:T(8,128)(2,1)}, u32[]{:S(2)}) copy-start(bf16[1,8,96,96]{3,2,0,1:T(8,128)(2,1)} %get-tuple-element.28) | copy-start | bytes 442372
  65.4 9.5 %copy-start.10 = (bf16[1,8,96,96]{3,2,0,1:T(8,128)(2,1)S(1)}, bf16[1,8,96,96]{3,2,0,1:T(8,128)(2,1)}, u32[]{:S(2)}) copy-start(bf16[1,8,96,96]{3,2,0,1:T(8,128)(2,1)} %get-tuple-element.29) | copy-start | bytes 442372
  65.4 9.5 %copy-start.11 = (bf16[1,8,96,96]{3,2,0,1:T(8,128)(2,1)S(1)}, bf16[1,8,96,96]{3,2,0,1:T(8,128)(2,1)}, u32[]{:S(2)}) copy-start(bf16[1,8,96,96]{3,2,0,1:T(8,128)(2,1)} %get-tuple-element.30) | copy-start | bytes 442372
  68.5 7.5 %copy-start.12 = (bf16[1,8,96,96]{3,2,0,1:T(8,128)(2,1)S(1)}, bf16[1,8,96,96]{3,2,0,1:T(8,128)(2,1)}, u32[]{:S(2)}) copy-start(bf16[1,8,96,96]{3,2,0,1:T(8,128)(2,1)} %get-tuple-element.33) | copy-start | bytes 442372
  68.5 7.5 %copy-start.13 = (bf16[1,8,96,96]{3,2,0,1:T(8,128)(2,1)S(1)}, bf16[1,8,96,96]{3,2,0,1:T(8,128)(2,1)}, u32[]{:S(2)}) copy-start(bf16[1,8,96,96]{3,2,0,1:T(8,128)(2,1)} %get-tuple-element.34) | copy-start | bytes 442372
  68.5 7.5 %copy-start.14 = (bf16[1,8,96,96]{3,2,0,1:T(8,128)(2,1)S(1)}, bf16[1,8,96,96]{3,2,0,1:T(8,128)(2,1)}, u32[]{:S(2)}) copy-start(bf16[1,8,96,96]{3,2,0,1:T(8,128)(2,1)} %get-tuple-element.35) | copy-start | bytes 442372
  68.5 16.5 %all-to-all-start.5 = ((bf16[16,2,9216]{2,1,0:T(2,128)(2,1)}), bf16[16,2,9216]{2,1,0:T(2,128)(2,1)}, u32[]{:S(2)}, u32[]{:S(2)}) async-start(bf16[16,2,9216]{2,1,0:T(2,128)(2,1)} %reshape.319), calls=%async_computation.5 | async-start | bytes 1179648 | tf_op jit(solution)/shard_map/all_to_all | solution.py:101
  80.6 1.6 copy-start.28
  80.6 1.6 copy-start.30
  89.7 2.9 copy-start.29
  89.7 2.9 copy-start.31
  89.7 2.9 copy-start.35
  92.6 1.2 copy-start.3
  93.8 1.9 copy-start.8
  94.3 1.4 copy-start.20
  94.3 1.4 copy-start.21
  97.0 1.3 copy-start.18
  97.0 1.3 copy-start.19
  98.8 1.2 copy-start.24
  98.8 1.2 copy-start.26
  103.7 8.2 %copy-start.5 = (bf16[2,8,96,96]{3,2,0,1:T(8,128)(2,1)S(1)}, bf16[2,8,96,96]{3,2,0,1:T(8,128)(2,1)}, u32[]{:S(2)}) copy-start(bf16[2,8,96,96]{3,2,0,1:T(8,128)(2,1)} %copy-done.4) | copy-start | bytes 884740
  106.7 19.5 %all-to-all-start.6 = ((bf16[16,2,9216]{2,1,0:T(2,128)(2,1)}), bf16[16,2,9216]{2,1,0:T(2,128)(2,1)}, u32[]{:S(2)}, u32[]{:S(2)}) async-start(bf16[16,2,9216]{2,1,0:T(2,128)(2,1)} %reshape.321), calls=%async_computation.6 | async-start | bytes 1179648 | tf_op jit(solution)/shard_map/all_to_all | solution.py:113
  113.6 1.2 copy-start.25
  113.6 1.2 copy-start.27
  113.7 1.2 copy-start.36
  124.7 7.6 %copy-start.6 = (f32[1,8,96,96]{2,3,1,0:T(8,128)S(1)}, f32[1,8,96,96]{2,3,1,0:T(8,128)}, u32[]{:S(2)}) copy-start(f32[1,8,96,96]{2,3,1,0:T(8,128)} %fusion.70) | copy-start | bytes 884740
  126.2 18.2 %all-to-all-start.2 = ((bf16[16,2,9216]{2,1,0:T(2,128)(2,1)}), bf16[16,2,9216]{2,1,0:T(2,128)(2,1)}, u32[]{:S(2)}, u32[]{:S(2)}) async-start(bf16[16,2,9216]{2,1,0:T(2,128)(2,1)} %reshape.313), calls=%async_computation.2 | async-start | bytes 1179648 | tf_op jit(solution)/shard_map/all_to_all | solution.py:113
  132.0 297.5 %all-reduce.5.cloned.1.call-start = ((), (), s32[]{:S(2)}) async-start(), calls=%async_computation.8 | async-start | bytes 3145728 | tf_op jit(solution)/shard_map/psum | solution.py:141
  136.7 1.2 copy-start.17
  144.4 17.9 %all-to-all-start.7 = ((bf16[16,2,9216]{2,1,0:T(2,128)(2,1)}), bf16[16,2,9216]{2,1,0:T(2,128)(2,1)}, u32[]{:S(2)}, u32[]{:S(2)}) async-start(bf16[16,2,9216]{2,1,0:T(2,128)(2,1)} %reshape.323), calls=%async_computation.7 | async-start | bytes 1179648 | tf_op jit(solution)/shard_map/all_to_all | solution.py:104
  162.3 271.7 %all-to-all-start.3 = ((bf16[16,2,9216]{2,1,0:T(2,128)(2,1)}), bf16[16,2,9216]{2,1,0:T(2,128)(2,1)}, u32[]{:S(2)}, u32[]{:S(2)}) async-start(bf16[16,2,9216]{2,1,0:T(2,128)(2,1)} %reshape.315), calls=%async_computation.3 | async-start | bytes 1179648 | tf_op jit(solution)/shard_map/all_to_all | solution.py:104
  167.4 418.7 %all-reduce.7.cloned.1.call-start = ((), (), s32[]{:S(2)}) async-start(), calls=%async_computation.9 | async-start | bytes 3145728 | tf_op jit(solution)/shard_map/psum | solution.py:141
  440.8 2.5 copy-start
  440.8 2.5 copy-start.2
  586.2 2.4 copy-start.7
Sparse Core Ops, SparseCore 0:
  136.4 293.1 all-reduce.4
  432.8 153.3 all-reduce.6
